TPU v7x, 256 devices: a whole 4x4x8 slice. The times are simulated.
256 devices in a mesh: row: 64 (over z, y, core), col: 4 (over x).
Axes of the slice: x: 4, y: 4, z: 8, core: 2. Of those that a mesh axis runs over, the one named last changes fastest.
Arguments:
- train_points: float32 [16, 3, 64, 128], P(None, None, 'row'), may hold values from -6 to 6
- new_points: float32 [16, 256], replicated, may hold values from -6 to 6
- lengthscales: float32 [16], replicated, may hold values from 2.5 to 6
- factor: float32 [3, 64, 128, 3, 4, 2048], P(None, 'row', None, None, 'col'), may hold values from -0.02734375 to 0.02734375
- diag_inverse: float32 [3, 64, 128, 4, 2048], P(None, 'row', None, 'col'), may hold values from -3 to 3
Outputs:
- solution: float32 [3, 4, 64, 32, 256], P(None, 'col', 'row')
All inputs are finite; a program needn't handle non-finite values.
Results may differ from a plain program's by a relative error of at most 0.0001.
Values sent between devices are 32-bit elements; how exact they have to be, the bound alone decides.
No kernel may reach another device: no remote copies, remote signals or barrier semaphores. Data moves between devices by JAX's collectives and lax.ppermute only.
A program may use at most 128 MiB of HBM per device.

v0:
```python
import jax
import jax.numpy as jnp
from jax import lax
from jax.sharding import PartitionSpec as P


def on_device(train_points, new_points, lengthscales, factor, diag_inverse):
    highest = lax.Precision.HIGHEST
    panels = factor.shape[0]
    block_rows = factor.shape[2]
    quarter_cols = factor.shape[5]
    new_count = new_points.shape[1]
    share_rows = block_rows // lax.axis_size("col")
    scaled_train = (train_points / lengthscales[:, None, None, None]).reshape(
        train_points.shape[0], panels * block_rows
    )
    scaled_new = new_points / lengthscales[:, None]
    inner_products = jnp.dot(scaled_train.T, scaled_new, precision=highest)
    sqdist = (
        jnp.sum(scaled_train * scaled_train, axis=0)[:, None]
        + jnp.sum(scaled_new * scaled_new, axis=0)[None, :]
        - 2.0 * inner_products
    )
    kernel = jnp.exp(-0.5 * sqdist).reshape(panels, block_rows, new_count)
    factor_blocks = factor.reshape(panels, block_rows, panels, quarter_cols)
    inverse_blocks = diag_inverse.reshape(panels, block_rows, quarter_cols)
    panel_numbers = jnp.arange(panels)

    def update(partial_rows, panel, quarter, after):
        column_slab = lax.dynamic_index_in_dim(factor_blocks, panel, axis=2, keepdims=False)
        change = jnp.einsum("piq,qm->pim", column_slab, quarter, precision=highest)
        below = (panel_numbers > after)[:, None, None]
        return partial_rows + jnp.where(below, change, 0.0)

    def advance(panel, loop_state):
        partial_rows, solved, pending = loop_state
        own_partial = lax.dynamic_index_in_dim(partial_rows, panel, 0, keepdims=False)
        summed = lax.psum(own_partial, "col")
        residual = lax.dynamic_index_in_dim(kernel, panel, 0, keepdims=False) - summed
        inverse_block = lax.dynamic_index_in_dim(inverse_blocks, panel, 0, keepdims=False)
        product = jnp.einsum("iq,im->qm", inverse_block, residual, precision=highest)
        own_rows = lax.psum_scatter(product, "row", scatter_dimension=0, tiled=True)
        quarter = lax.all_gather(own_rows, "row", axis=0, tiled=True)
        solved = lax.dynamic_update_index_in_dim(solved, own_rows, panel, 0)
        partial_rows = update(partial_rows, panel, quarter, panel)
        return (partial_rows, solved, pending)

    initial = (
        jnp.zeros((panels, block_rows, new_count), jnp.float32),
        jnp.zeros((panels, share_rows, new_count), jnp.float32),
        jnp.zeros((quarter_cols, new_count), jnp.float32),
    )
    partial_rows, solved, pending = lax.fori_loop(0, panels, advance, initial)
    return solved.reshape(panels, 1, 1, share_rows, new_count)


def solution(mesh):
    return jax.shard_map(
        on_device,
        mesh=mesh,
        in_specs=(
            P(None, None, "row", None),
            P(),
            P(),
            P(None, "row", None, None, "col", None),
            P(None, "row", None, "col", None),
        ),
        out_specs=P(None, "col", "row", None, None),
        check_vma=False,
    )
```

profile of v0, /device:TPU:1, one launch (start us, length us, event | category | flops | bytes accessed | tf_op | source)
XLA Modules:
  0.0 868.2 jit_solution(1024487664733539460)
XLA Ops:
  6.5 0.9 fusion.27
  7.4 0.8 multiply_reduce_fusion.1
  8.3 2.0 fusion.24
  10.3 12.1 %copy.15 = f32[3,1,128,3,1,2048]{5,2,0,3,4,1:T(8,128)} copy(f32[3,1,128,3,1,2048]{5,4,3,2,1,0:T(1,128)} %param.10) | data formatting | bytes 18874368 | tf_op args[3]
  22.4 0.0 copy-done
  22.4 1.4 copy.16
  23.8 837.8 %while.16 = (s32[]{:T(128)}, f32[3,128,256]{2,1,0:T(8,128)}, f32[3,32,256]{2,1,0:T(8,128)}, f32[3,128,3,2048]{3,1,0,2:T(8,128)}, f32[3,128,2048]{2,1,0:T(8,128)S...) while((s32[]{:T(128)}, f32[3,128,256]{2,1,0:T(8,128)}, f32[3,32,256]{2,1,0:T(8,128)}, ...), condition=%wide.region_5.6_spmd.clone, body=%wide.region_2.5_spmd.clone.sunk | while | flops 3221585920 | bytes 24118516 | solution.py:53
  24.0 0.0 all-reduce.2.cloned.1.call-start
  24.1 0.7 dynamic-slice_bitcast_fusion.2
  24.8 0.0 all-reduce.2.cloned.1.call-update
  24.8 0.0 reduce-scatter.2.cloned.1.call-start
  24.9 50.3 %all-reduce.2.cloned.1.call-done = f32[128,256]{1,0:T(8,128)} async-done(((f32[128,256]{1,0:T(8,128)}), f32[128,256]{1,0:T(8,128)}) %all-reduce.2.cloned.1.call-update) | async-done | bytes 131088 | tf_op jit(solution)/shard_map/while/body/eval_jaxpr/psum | solution.py:38
  75.2 4.1 fusion.36
  79.3 0.0 reduce-scatter.2.cloned.1.call-update
  79.3 0.0 all-gather.2.cloned.1.call-start
  79.4 138.6 %reduce-scatter.2.cloned.1.call-done = f32[32,256]{1,0:T(8,128)} async-done(((f32[2048,256]{1,0:T(8,128)}), f32[32,256]{1,0:T(8,128)}) %reduce-scatter.2.cloned.1.call-update) | async-done | bytes 32784 | tf_op jit(solution)/shard_map/while/body/eval_jaxpr/reduce_scatter | solution.py:42
  218.0 0.0 all-gather.2.cloned.1.call-update
  218.1 1.4 bitcast_dynamic-update-slice_fusion.2
  219.4 82.4 %all-gather.2.cloned.1.call-done = f32[2048,256]{1,0:T(8,128)} async-done(((f32[32,256]{1,0:T(8,128)}), f32[2048,256]{1,0:T(8,128)}) %all-gather.2.cloned.1.call-update) | async-done | bytes 2097168 | tf_op jit(solution)/shard_map/while/body/eval_jaxpr/all_gather | solution.py:43
  301.9 6.0 fusion.37
  307.8 0.0 all-reduce.2.cloned.1.call-start
  307.8 1.0 broadcast_select_fusion.2
  308.9 0.7 dynamic-slice_bitcast_fusion.2
  309.5 0.0 all-reduce.2.cloned.1.call-update
  309.6 0.0 reduce-scatter.2.cloned.1.call-start
  309.6 42.5 %all-reduce.2.cloned.1.call-done = f32[128,256]{1,0:T(8,128)} async-done(((f32[128,256]{1,0:T(8,128)}), f32[128,256]{1,0:T(8,128)}) %all-reduce.2.cloned.1.call-update) | async-done | bytes 131088 | tf_op jit(solution)/shard_map/while/body/eval_jaxpr/psum | solution.py:38
  352.1 4.1 fusion.36
  356.2 0.0 reduce-scatter.2.cloned.1.call-update
  356.2 0.0 all-gather.2.cloned.1.call-start
  356.3 138.2 %reduce-scatter.2.cloned.1.call-done = f32[32,256]{1,0:T(8,128)} async-done(((f32[2048,256]{1,0:T(8,128)}), f32[32,256]{1,0:T(8,128)}) %reduce-scatter.2.cloned.1.call-update) | async-done | bytes 32784 | tf_op jit(solution)/shard_map/while/body/eval_jaxpr/reduce_scatter | solution.py:42
  494.5 0.0 all-gather.2.cloned.1.call-update
  494.5 1.4 bitcast_dynamic-update-slice_fusion.2
  495.9 82.6 %all-gather.2.cloned.1.call-done = f32[2048,256]{1,0:T(8,128)} async-done(((f32[32,256]{1,0:T(8,128)}), f32[2048,256]{1,0:T(8,128)}) %all-gather.2.cloned.1.call-update) | async-done | bytes 2097168 | tf_op jit(solution)/shard_map/while/body/eval_jaxpr/all_gather | solution.py:43
  578.5 6.0 fusion.37
  584.4 0.0 all-reduce.2.cloned.1.call-start
  584.5 1.0 broadcast_select_fusion.2
  585.5 0.7 dynamic-slice_bitcast_fusion.2
  586.1 0.0 all-reduce.2.cloned.1.call-update
  586.2 0.0 reduce-scatter.2.cloned.1.call-start
  586.2 42.8 %all-reduce.2.cloned.1.call-done = f32[128,256]{1,0:T(8,128)} async-done(((f32[128,256]{1,0:T(8,128)}), f32[128,256]{1,0:T(8,128)}) %all-reduce.2.cloned.1.call-update) | async-done | bytes 131088 | tf_op jit(solution)/shard_map/while/body/eval_jaxpr/psum | solution.py:38
  629.0 4.1 fusion.36
  633.2 0.0 reduce-scatter.2.cloned.1.call-update
  633.2 0.0 all-gather.2.cloned.1.call-start
  633.2 138.6 %reduce-scatter.2.cloned.1.call-done = f32[32,256]{1,0:T(8,128)} async-done(((f32[2048,256]{1,0:T(8,128)}), f32[32,256]{1,0:T(8,128)}) %reduce-scatter.2.cloned.1.call-update) | async-done | bytes 32784 | tf_op jit(solution)/shard_map/while/body/eval_jaxpr/reduce_scatter | solution.py:42
  771.9 0.0 all-gather.2.cloned.1.call-update
  771.9 1.4 bitcast_dynamic-update-slice_fusion.2
  773.3 82.4 %all-gather.2.cloned.1.call-done = f32[2048,256]{1,0:T(8,128)} async-done(((f32[32,256]{1,0:T(8,128)}), f32[2048,256]{1,0:T(8,128)}) %all-gather.2.cloned.1.call-update) | async-done | bytes 2097168 | tf_op jit(solution)/shard_map/while/body/eval_jaxpr/all_gather | solution.py:43
  855.7 6.0 fusion.37
  (7 shorter events, 0.1 us)
Async XLA Ops:
  10.3 12.1 %copy-start = (f32[3,1,128,1,2048]{4,3,2,1,0:T(1,128)S(1)}, f32[3,1,128,1,2048]{4,3,2,1,0:T(1,128)}, u32[]{:S(2)}) copy-start(f32[3,1,128,1,2048]{4,3,2,1,0:T(1,128)} %param.11) | copy-start | bytes 9437188
  24.0 51.2 %all-reduce.2.cloned.1.call-start = ((), (), s32[]{:S(2)}) async-start(), calls=%async_computation.1 | async-start | bytes 262144 | tf_op jit(solution)/shard_map/while/body/eval_jaxpr/psum | solution.py:38
  24.8 193.2 %reduce-scatter.2.cloned.1.call-start = ((), (), s32[]{:S(2)}) async-start(), calls=%async_computation.2 | async-start | bytes 2129920 | tf_op jit(solution)/shard_map/while/body/eval_jaxpr/reduce_scatter | solution.py:42
  79.3 222.5 %all-gather.2.cloned.1.call-start = ((), (), s32[]{:S(2)}) async-start(), calls=%async_computation.3 | async-start | bytes 2129920 | tf_op jit(solution)/shard_map/while/body/eval_jaxpr/all_gather | solution.py:43
  307.8 44.3 %all-reduce.2.cloned.1.call-start = ((), (), s32[]{:S(2)}) async-start(), calls=%async_computation.1 | async-start | bytes 262144 | tf_op jit(solution)/shard_map/while/body/eval_jaxpr/psum | solution.py:38
  309.6 184.9 %reduce-scatter.2.cloned.1.call-start = ((), (), s32[]{:S(2)}) async-start(), calls=%async_computation.2 | async-start | bytes 2129920 | tf_op jit(solution)/shard_map/while/body/eval_jaxpr/reduce_scatter | solution.py:42
  356.2 222.2 %all-gather.2.cloned.1.call-start = ((), (), s32[]{:S(2)}) async-start(), calls=%async_computation.3 | async-start | bytes 2129920 | tf_op jit(solution)/shard_map/while/body/eval_jaxpr/all_gather | solution.py:43
  584.4 44.6 %all-reduce.2.cloned.1.call-start = ((), (), s32[]{:S(2)}) async-start(), calls=%async_computation.1 | async-start | bytes 262144 | tf_op jit(solution)/shard_map/while/body/eval_jaxpr/psum | solution.py:38
  586.2 185.7 %reduce-scatter.2.cloned.1.call-start = ((), (), s32[]{:S(2)}) async-start(), calls=%async_computation.2 | async-start | bytes 2129920 | tf_op jit(solution)/shard_map/while/body/eval_jaxpr/reduce_scatter | solution.py:42
  633.2 222.5 %all-gather.2.cloned.1.call-start = ((), (), s32[]{:S(2)}) async-start(), calls=%async_computation.3 | async-start | bytes 2129920 | tf_op jit(solution)/shard_map/while/body/eval_jaxpr/all_gather | solution.py:43
Sparse Core Ops, SparseCore 0:
  27.2 47.9 all-reduce.1
  79.8 138.1 reduce-scatter.1
  220.8 81.0 all-gather.1
  310.7 41.4 all-reduce.1
  356.6 137.9 reduce-scatter.1
  497.1 81.3 all-gather.1
  587.6 41.4 all-reduce.1
  633.6 138.1 reduce-scatter.1
  774.6 81.0 all-gather.1
where the time goes:
time: 869 us; the launch traced here: 868 us
  waiting for transfers between devices  799 us (92%)
  matrix products  32.3 us (4%)
  local copies, waits for them, and re-layouts  19.7 us (2%)
  between operations  13.1 us (2%)
    reduce_scatter x3, waiting for transfers between devices, advance(): own_rows = lax.psum_scatter(product, 'row', scatter_dimension=0, tiled=True)  415 us
    all_gather x3, waiting for transfers between devices, advance(): quarter = lax.all_gather(own_rows, 'row', axis=0, tiled=True)  247 us
    psum x3, waiting for transfers between devices, advance(): summed = lax.psum(own_partial, 'col')  136 us
    dot_general x3, matrix products, update(): change = jnp.einsum('piq,qm->pim', column_slab, quarter, precision=highest)  17.9 us
  transfers between devices with their start and end apart: 9, of which 9 were waited for; matrix products, arithmetic and copies ran while one was open for 0% of the time, Pallas kernels for 0%

commit v1 on v0

--- a/solution.py
+++ b/solution.py
@@ -35,7 +35,7 @@
     def advance(panel, loop_state):
         partial_rows, solved, pending = loop_state
         own_partial = lax.dynamic_index_in_dim(partial_rows, panel, 0, keepdims=False)
-        summed = lax.psum(own_partial, "col")
+        summed = jnp.sum(lax.all_gather(own_partial, "col"), axis=0)
         residual = lax.dynamic_index_in_dim(kernel, panel, 0, keepdims=False) - summed
         inverse_block = lax.dynamic_index_in_dim(inverse_blocks, panel, 0, keepdims=False)
         product = jnp.einsum("iq,im->qm", inverse_block, residual, precision=highest)

time: 869 us -> 759 us (0.87)
  waiting for transfers between devices: 799 us -> 659 us
  blocking collectives: 0 us -> 34.2 us
    psum x3 -> x0, waiting for transfers between devices: 136 us -> none  [advance(): summed = lax.psum(own_partial, 'col')]
    all_gather x0 -> x3, blocking collectives: none -> 34.2 us  [advance(): summed = jnp.sum(lax.all_gather(own_partial, 'col'), axis=0)]
  transfers between devices with their start and end apart: 9 -> 6, of which waited for: 9 -> 6; matrix products, arithmetic and copies ran while one was open for 0% -> 1% of each run, Pallas kernels for 0% -> 0%
where the time goes in v1:
time: 759 us; the launch traced here: 758 us
  waiting for transfers between devices  659 us (87%)
  blocking collectives  34.2 us (5%)
  matrix products  30.1 us (4%)
  local copies, waits for them, and re-layouts  19.4 us (3%)
  between operations  13.4 us (2%)
    reduce_scatter x3, waiting for transfers between devices, advance(): own_rows = lax.psum_scatter(product, 'row', scatter_dimension=0, tiled=True)  410 us
    all_gather x3, waiting for transfers between devices, advance(): quarter = lax.all_gather(own_rows, 'row', axis=0, tiled=True)  249 us
    all_gather x3, blocking collectives, advance(): summed = jnp.sum(lax.all_gather(own_partial, 'col'), axis=0)  34.2 us
    dot_general x3, matrix products, update(): change = jnp.einsum('piq,qm->pim', column_slab, quarter, precision=highest)  15.6 us
  transfers between devices with their start and end apart: 6, of which 6 were waited for; matrix products, arithmetic and copies ran while one was open for 1% of the time, Pallas kernels for 0%

profile of v1, /device:TPU:1, one launch (start us, length us, event | category | flops | bytes accessed | tf_op | source)
XLA Modules:
  0.0 758.5 jit_solution(3933065390499230057)
XLA Ops:
  6.5 0.9 fusion.28
  7.4 0.8 multiply_reduce_fusion.1
  8.3 1.3 fusion.25
  9.5 0.0 copy-start
  9.6 12.1 %copy.16 = f32[3,1,128,3,1,2048]{5,2,0,3,4,1:T(8,128)} copy(f32[3,1,128,3,1,2048]{5,4,3,2,1,0:T(1,128)} %param.10) | data formatting | bytes 18874368 | tf_op args[3]
  21.7 0.0 copy-done
  21.7 3.0 copy.17
  24.7 726.9 %while.16 = (s32[]{:T(128)}, f32[3,128,256]{2,1,0:T(8,128)S(1)}, f32[3,32,256]{2,1,0:T(8,128)}, f32[3,128,3,2048]{3,1,0,2:T(8,128)}, f32[3,128,2048]{2,1,0:T(8,1...) while((s32[]{:T(128)}, f32[3,128,256]{2,1,0:T(8,128)S(1)}, ...), condition=%wide.region_5.6_spmd.clone, body=%wide.region_2.5_spmd.clone.sunk | while | flops 3221651456 | bytes 24642776 | solution.py:53
  24.7 0.0 reduce-scatter.2.cloned.1.call-start
  24.8 12.3 %all_gather.19 = f32[4,128,256]{2,1,0:T(8,128)S(1)} all-gather(f32[1,128,256]{2,1,0:T(8,128)S(1)} %constant_dynamic-slice_fusion.2), channel_id=1, replica_groups=mesh['row'=64,'col'=4] {'col'}, dimensions={0}, use_global_device_ids=true | all-gather | bytes 655360 | tf_op jit(solution)/shard_map/while/body/eval_jaxpr/all_gather | solution.py:38
  37.1 4.4 fusion.39
  41.6 0.0 reduce-scatter.2.cloned.1.call-update
  41.6 0.0 all-gather.2.cloned.1.call-start
  41.6 140.4 %reduce-scatter.2.cloned.1.call-done = f32[32,256]{1,0:T(8,128)} async-done(((f32[2048,256]{1,0:T(8,128)}), f32[32,256]{1,0:T(8,128)}) %reduce-scatter.2.cloned.1.call-update) | async-done | bytes 32784 | tf_op jit(solution)/shard_map/while/body/eval_jaxpr/reduce_scatter | solution.py:42
  182.0 0.0 all-gather.2.cloned.1.call-update
  182.0 1.4 bitcast_dynamic-update-slice_fusion.2
  183.4 82.8 %all-gather.2.cloned.1.call-done = f32[2048,256]{1,0:T(8,128)} async-done(((f32[32,256]{1,0:T(8,128)}), f32[2048,256]{1,0:T(8,128)}) %all-gather.2.cloned.1.call-update) | async-done | bytes 2097168 | tf_op jit(solution)/shard_map/while/body/eval_jaxpr/all_gather | solution.py:43
  266.3 5.2 fusion.40
  271.5 0.0 reduce-scatter.2.cloned.1.call-start
  271.6 10.9 %all_gather.19 = f32[4,128,256]{2,1,0:T(8,128)S(1)} all-gather(f32[1,128,256]{2,1,0:T(8,128)S(1)} %constant_dynamic-slice_fusion.2), channel_id=1, replica_groups=mesh['row'=64,'col'=4] {'col'}, dimensions={0}, use_global_device_ids=true | all-gather | bytes 655360 | tf_op jit(solution)/shard_map/while/body/eval_jaxpr/all_gather | solution.py:38
  282.6 4.4 fusion.39
  287.0 0.0 reduce-scatter.2.cloned.1.call-update
  287.0 0.0 all-gather.2.cloned.1.call-start
  287.1 135.1 %reduce-scatter.2.cloned.1.call-done = f32[32,256]{1,0:T(8,128)} async-done(((f32[2048,256]{1,0:T(8,128)}), f32[32,256]{1,0:T(8,128)}) %reduce-scatter.2.cloned.1.call-update) | async-done | bytes 32784 | tf_op jit(solution)/shard_map/while/body/eval_jaxpr/reduce_scatter | solution.py:42
  422.2 0.0 all-gather.2.cloned.1.call-update
  422.2 1.4 bitcast_dynamic-update-slice_fusion.2
  423.6 82.8 %all-gather.2.cloned.1.call-done = f32[2048,256]{1,0:T(8,128)} async-done(((f32[32,256]{1,0:T(8,128)}), f32[2048,256]{1,0:T(8,128)}) %all-gather.2.cloned.1.call-update) | async-done | bytes 2097168 | tf_op jit(solution)/shard_map/while/body/eval_jaxpr/all_gather | solution.py:43
  506.3 5.2 fusion.40
  511.6 0.0 reduce-scatter.2.cloned.1.call-start
  511.7 10.9 %all_gather.19 = f32[4,128,256]{2,1,0:T(8,128)S(1)} all-gather(f32[1,128,256]{2,1,0:T(8,128)S(1)} %constant_dynamic-slice_fusion.2), channel_id=1, replica_groups=mesh['row'=64,'col'=4] {'col'}, dimensions={0}, use_global_device_ids=true | all-gather | bytes 655360 | tf_op jit(solution)/shard_map/while/body/eval_jaxpr/all_gather | solution.py:38
  522.7 4.4 fusion.39
  527.1 0.0 reduce-scatter.2.cloned.1.call-update
  527.1 0.0 all-gather.2.cloned.1.call-start
  527.2 134.7 %reduce-scatter.2.cloned.1.call-done = f32[32,256]{1,0:T(8,128)} async-done(((f32[2048,256]{1,0:T(8,128)}), f32[32,256]{1,0:T(8,128)}) %reduce-scatter.2.cloned.1.call-update) | async-done | bytes 32784 | tf_op jit(solution)/shard_map/while/body/eval_jaxpr/reduce_scatter | solution.py:42
  661.9 0.0 all-gather.2.cloned.1.call-update
  662.0 1.4 bitcast_dynamic-update-slice_fusion.2
  663.3 83.1 %all-gather.2.cloned.1.call-done = f32[2048,256]{1,0:T(8,128)} async-done(((f32[32,256]{1,0:T(8,128)}), f32[2048,256]{1,0:T(8,128)}) %all-gather.2.cloned.1.call-update) | async-done | bytes 2097168 | tf_op jit(solution)/shard_map/while/body/eval_jaxpr/all_gather | solution.py:43
  746.4 5.2 fusion.40
  (14 shorter events, 0.3 us)
Async XLA Ops:
  9.5 12.1 %copy-start = (f32[3,1,128,1,2048]{4,3,2,1,0:T(1,128)S(1)}, f32[3,1,128,1,2048]{4,3,2,1,0:T(1,128)}, u32[]{:S(2)}) copy-start(f32[3,1,128,1,2048]{4,3,2,1,0:T(1,128)} %param.11) | copy-start | bytes 9437188
  24.7 157.3 %reduce-scatter.2.cloned.1.call-start = ((), (), s32[]{:S(2)}) async-start(), calls=%async_computation.1 | async-start | bytes 2129920 | tf_op jit(solution)/shard_map/while/body/eval_jaxpr/reduce_scatter | solution.py:42
  41.6 224.7 %all-gather.2.cloned.1.call-start = ((), (), s32[]{:S(2)}) async-start(), calls=%async_computation.2 | async-start | bytes 2129920 | tf_op jit(solution)/shard_map/while/body/eval_jaxpr/all_gather | solution.py:43
  271.5 150.7 %reduce-scatter.2.cloned.1.call-start = ((), (), s32[]{:S(2)}) async-start(), calls=%async_computation.1 | async-start | bytes 2129920 | tf_op jit(solution)/shard_map/while/body/eval_jaxpr/reduce_scatter | solution.py:42
  287.0 219.3 %all-gather.2.cloned.1.call-start = ((), (), s32[]{:S(2)}) async-start(), calls=%async_computation.2 | async-start | bytes 2129920 | tf_op jit(solution)/shard_map/while/body/eval_jaxpr/all_gather | solution.py:43
  511.6 150.3 %reduce-scatter.2.cloned.1.call-start = ((), (), s32[]{:S(2)}) async-start(), calls=%async_computation.1 | async-start | bytes 2129920 | tf_op jit(solution)/shard_map/while/body/eval_jaxpr/reduce_scatter | solution.py:42
  527.1 219.3 %all-gather.2.cloned.1.call-start = ((), (), s32[]{:S(2)}) async-start(), calls=%async_computation.2 | async-start | bytes 2129920 | tf_op jit(solution)/shard_map/while/body/eval_jaxpr/all_gather | solution.py:43
Sparse Core Ops, SparseCore 0:
  41.7 140.2 reduce-scatter.1
  185.2 81.0 all-gather.1
  287.2 134.9 reduce-scatter.1
  425.2 81.1 all-gather.1
  527.2 134.6 reduce-scatter.1
  664.9 81.4 all-gather.1
